TPU v7x, 512 devices: a whole 4x4x16 slice. The times are simulated.
512 devices in a mesh: group: 8 (over z_lo), shard: 64 (over z_hi, x, y, core).
Axes of the slice: x: 4, y: 4, z: 16 (z_hi: 2, z_lo: 8; z = z_hi * 8 + z_lo), core: 2. Of those that a mesh axis runs over, the one named last changes fastest.
Arguments:
- inner_embed: float32 [8, 15360, 768], P('group', 'shard'), may hold values from -6 to 6
- outer_embed: float32 [15360, 768], P('shard'), may hold values from -6 to 6
- moment_embed: float32 [15360, 768], P('shard'), may hold values from -6 to 6
- basis: float32 [15360, 64], P('shard'), may hold values from -6 to 6
- inner_attn: float32 [8, 768, 3072], P('group', 'shard'), may hold values from -6 to 6
- outer_attn: float32 [768, 3072], P(None, 'shard'), may hold values from -6 to 6
- moment_attn: float32 [768, 3072], P(None, 'shard'), may hold values from -6 to 6
- inner_norms: float32 [8, 4, 768], P('group', None, 'shard'), may hold values from -6 to 6
- outer_norms: float32 [4, 768], P(None, 'shard'), may hold values from -6 to 6
- moment_norms: float32 [4, 768], P(None, 'shard'), may hold values from -6 to 6
Outputs:
- new_embed: float32 [15360, 768], P('shard')
- new_moment_embed: float32 [15360, 768], P('shard')
- new_attn: float32 [768, 3072], P(None, 'shard')
- new_moment_attn: float32 [768, 3072], P(None, 'shard')
- new_norms: float32 [4, 768], P(None, 'shard')
- new_moment_norms: float32 [4, 768], P(None, 'shard')
- replica_attn: bfloat16 [768, 3072], P('shard')
All inputs are finite; a program needn't handle non-finite values.
Results may differ from a plain program's by a relative error of at most 0.0004.
Values may be sent and summed in bfloat16 or wider, within the bound.
A program may use at most 64 MiB of HBM per device.

v0:
```python
import math
import jax
import jax.numpy as jnp
from jax import lax
from jax.sharding import PartitionSpec as P

VOCAB = 15360
RANK = 64


def nesterov(outer, moment, delta):
    moment_new = 0.5 * moment + delta
    return (outer - (delta + 0.5 * moment_new), moment_new)


def on_device(
    inner_embed,
    outer_embed,
    moment_embed,
    basis,
    inner_attn,
    outer_attn,
    moment_attn,
    inner_norms,
    outer_norms,
    moment_norms,
):
    groups = lax.axis_size("group")
    embed_diff = outer_embed - inner_embed[0]
    partial_coeff = lax.dot_general(
        basis,
        embed_diff,
        (((0,), (0,)), ((), ())),
        precision=lax.Precision.HIGHEST,
        preferred_element_type=jnp.float32,
    )
    norm_diff = outer_norms - inner_norms[0]
    moved = lax.all_to_all(inner_attn[0], "shard", split_axis=1, concat_axis=0, tiled=True)
    attn_term = outer_attn - moved
    coeff_sum = lax.psum(partial_coeff, ("group", "shard"))
    attn_sum, norm_sum = lax.psum((attn_term, norm_diff), "group")
    attn_delta = attn_sum / groups
    norm_delta = norm_sum / groups
    coefficient = coeff_sum / groups
    embed_delta = jnp.dot(
        basis, coefficient, precision=lax.Precision.HIGHEST, preferred_element_type=jnp.float32
    ) * (1.0 / math.sqrt(RANK * VOCAB))
    new_embed, new_moment_embed = nesterov(outer_embed, moment_embed, embed_delta)
    new_attn, new_moment_attn = nesterov(outer_attn, moment_attn, attn_delta)
    new_norms, new_moment_norms = nesterov(outer_norms, moment_norms, norm_delta)
    replica_attn = lax.all_to_all(
        new_attn.astype(jnp.bfloat16), "shard", split_axis=0, concat_axis=1, tiled=True
    )
    return (
        new_embed,
        new_moment_embed,
        new_attn,
        new_moment_attn,
        new_norms,
        new_moment_norms,
        replica_attn,
    )


def solution(mesh):
    placed = (
        P("group", "shard", None),
        P("shard", None),
        P("shard", None),
        P("shard", None),
        P("group", "shard", None),
        P(None, "shard"),
        P(None, "shard"),
        P("group", None, "shard"),
        P(None, "shard"),
        P(None, "shard"),
    )
    return jax.shard_map(
        on_device,
        mesh=mesh,
        in_specs=placed,
        out_specs=(
            P("shard", None),
            P("shard", None),
            P(None, "shard"),
            P(None, "shard"),
            P(None, "shard"),
            P(None, "shard"),
            P("shard", None),
        ),
        check_vma=False,
    )
```

profile of v0, /device:TPU:1, one launch (start us, length us, event | category | flops | bytes accessed | tf_op | source)
XLA Modules:
  0.0 638.4 jit_solution(14730503204910227283)
XLA Ops:
  7.2 0.0 copy-start
  7.2 1.3 reduce
  8.5 0.2 all_to_all.28
  8.7 0.2 copy.34
  8.9 1.0 reshape.22
  9.9 0.0 copy-start.4
  9.9 22.4 %all-to-all-start = ((f32[64,1,576]{2,1,0:T(1,128)}), f32[64,1,576]{2,1,0:T(1,128)S(1)}, u32[]{:S(2)}, u32[]{:S(2)}) async-start(f32[64,1,576]{2,1,0:T(1,128)} %reshape.22), calls=%async_computation | async-start | bytes 327680 | tf_op jit(solution)/shard_map/all_to_all | solution.py:38
  32.3 0.0 all-reduce.5.cloned.1.call-start
  32.4 0.0 copy-done.4
  32.4 0.2 copy.29
  32.6 17.3 %all-to-all-done = f32[64,1,576]{2,1,0:T(1,128)S(1)} async-done(((f32[64,1,576]{2,1,0:T(1,128)}), f32[64,1,576]{2,1,0:T(1,128)S(1)}, u32[]{:S(2)}, u32[]{:S(2)}) %all-to-all-start) | async-done | bytes 147488 | tf_op jit(solution)/shard_map/all_to_all | solution.py:38
  49.9 0.5 broadcast.29
  50.4 1.0 reduce.1
  51.4 0.2 reshape.23
  51.7 0.0 copy-start.1
  51.7 0.0 copy-start.2
  51.7 0.8 sub.20
  52.5 0.0 all-reduce.5.cloned.1.call-update
  52.5 0.0 all-reduce.3.cloned.1.call-start
  52.6 0.0 copy-done
  52.6 0.4 copy-done.1
  53.0 0.2 copy-done.2
  53.2 1.3 convolution_bitcast_fusion
  54.5 0.0 copy-start.5
  54.5 0.0 all-reduce.3.cloned.1.call-update
  54.5 0.9 copy-done.5
  55.4 0.0 copy-start.6
  55.4 0.0 copy-start.7
  55.4 0.2 copy.28
  55.5 0.5 copy-done.6
  56.1 0.0 copy-done.7
  56.1 0.0 copy-start.8
  56.1 27.7 %psum.23 = f32[4,12]{1,0:T(4,128)S(1)} all-reduce(f32[4,12]{1,0:T(4,128)S(1)} %bitcast_subtract_fusion.2), channel_id=1, replica_groups=mesh['group'=8,'shard'=64] {'group'}, use_global_device_ids=true, to_apply=%region_2.0 | all-reduce | flops 48 | bytes 384 | tf_op jit(solution)/shard_map/psum | solution.py:41
  83.8 0.0 copy-done.8
  83.8 0.6 add_subtract_fusion.2
  84.4 80.6 %all-reduce.5.cloned.1.call-done = f32[768,48]{1,0:T(8,128)} async-done(((f32[768,48]{1,0:T(8,128)}), f32[768,48]{1,0:T(8,128)}) %all-reduce.5.cloned.1.call-update) | async-done | bytes 147472 | tf_op jit(solution)/shard_map/psum | solution.py:41
  165.0 1.1 fusion.4
  166.1 0.0 copy-start.3
  166.1 0.1 all_to_all.32
  166.2 0.9 reshape.24
  167.1 16.1 %all-to-all-start.1 = ((bf16[64,2,288]{2,1,0:T(2,128)(2,1)}), bf16[64,2,288]{2,1,0:T(2,128)(2,1)S(1)}, u32[]{:S(2)}, u32[]{:S(2)}) async-start(bf16[64,2,288]{2,1,0:T(2,128)(2,1)} %reshape.24), calls=%async_computation.1 | async-start | bytes 196608 | tf_op jit(solution)/shard_map/all_to_all | solution.py:51
  183.3 442.5 %all-reduce.3.cloned.1.call-done = f32[64,768]{1,0:T(8,128)} async-done(((f32[64,768]{1,0:T(8,128)}), f32[64,768]{1,0:T(8,128)}) %all-reduce.3.cloned.1.call-update) | async-done | bytes 196624 | tf_op jit(solution)/shard_map/psum | solution.py:40
  625.8 0.0 copy-done.3
  625.8 2.9 add_subtract_fusion
  628.7 0.8 copy.31
  629.5 0.8 copy.32
  630.3 0.0 all-to-all-done.1
  630.3 0.2 reshape.25
  630.6 0.1 copy.30
  630.6 0.9 all_to_all.35
  (3 shorter events, 0.1 us)
Async XLA Ops:
  7.2 45.4 %copy-start = (f32[240,64]{0,1:T(8,128)S(1)}, f32[240,64]{0,1:T(8,128)}, u32[]{:S(2)}) copy-start(f32[240,64]{0,1:T(8,128)} %param.13) | copy-start | bytes 184324
  9.9 22.4 %copy-start.4 = (f32[768,48]{0,1:T(8,128)S(1)}, f32[768,48]{0,1:T(8,128)}, u32[]{:S(2)}) copy-start(f32[768,48]{0,1:T(8,128)} %param.15) | copy-start | bytes 442372
  9.9 39.9 %all-to-all-start = ((f32[64,1,576]{2,1,0:T(1,128)}), f32[64,1,576]{2,1,0:T(1,128)S(1)}, u32[]{:S(2)}, u32[]{:S(2)}) async-start(f32[64,1,576]{2,1,0:T(1,128)} %reshape.22), calls=%async_computation | async-start | bytes 327680 | tf_op jit(solution)/shard_map/all_to_all | solution.py:38
  32.3 132.7 %all-reduce.5.cloned.1.call-start = ((), (), s32[]{:S(2)}) async-start(), calls=%async_computation.3 | async-start | bytes 786432 | tf_op jit(solution)/shard_map/psum | solution.py:41
  51.7 1.3 copy-start.1
  51.7 1.5 copy-start.2
  52.5 573.3 %all-reduce.3.cloned.1.call-start = ((), (), s32[]{:S(2)}) async-start(), calls=%async_computation.2 | async-start | bytes 393216 | tf_op jit(solution)/shard_map/psum | solution.py:40
  54.5 0.9 copy-start.5
  55.4 0.7 copy-start.6
  55.4 0.7 copy-start.7
  56.1 27.7 %copy-start.8 = (f32[4,12]{1,0:T(4,128)S(1)}, f32[4,12]{1,0:T(4,128)}, u32[]{:S(2)}) copy-start(f32[4,12]{1,0:T(4,128)} %param.19) | copy-start | bytes 580
  166.1 459.7 %copy-start.3 = (f32[240,768]{1,0:T(8,128)S(1)}, f32[240,768]{1,0:T(8,128)}, u32[]{:S(2)}) copy-start(f32[240,768]{1,0:T(8,128)} %param.12) | copy-start | bytes 2211844
  167.1 463.2 %all-to-all-start.1 = ((bf16[64,2,288]{2,1,0:T(2,128)(2,1)}), bf16[64,2,288]{2,1,0:T(2,128)(2,1)S(1)}, u32[]{:S(2)}, u32[]{:S(2)}) async-start(bf16[64,2,288]{2,1,0:T(2,128)(2,1)} %reshape.24), calls=%async_computation.1 | async-start | bytes 196608 | tf_op jit(solution)/shard_map/all_to_all | solution.py:51
Sparse Core Ops, SparseCore 0:
  52.7 112.3 all-reduce.4
  171.9 453.8 all-reduce.2
where the time goes:
time: 639 us; the launch traced here: 638 us
  waiting for transfers between devices  540 us (85%)
  starting transfers between devices  38.6 us (6%)
  blocking collectives  27.7 us (4%)
  between operations  14.2 us (2%)
  local copies, waits for them, and re-layouts  8.4 us (1%)
    psum x1, waiting for transfers between devices, on_device(): coeff_sum = lax.psum(partial_coeff, ('group', 'shard'))  442 us
    psum x1, waiting for transfers between devices, on_device(): attn_sum, norm_sum = lax.psum((attn_term, norm_diff), 'group')  80.6 us
    psum x1, blocking collectives, on_device(): attn_sum, norm_sum = lax.psum((attn_term, norm_diff), 'group')  27.7 us
    all_to_all x1, starting transfers between devices, on_device(): lax.all_to_all(inner_attn[0], 'shard', split_axis=1, concat_axis=0, tiled...  22.4 us
    all_to_all x1, waiting for transfers between devices, on_device(): lax.all_to_all(inner_attn[0], 'shard', split_axis=1, concat_axis=0, tiled...  17.3 us
    all_to_all x1, starting transfers between devices, on_device(): lax.all_to_all(new_attn.astype(jnp.bfloat16), 'shard', split_axis=0, conc...  16.1 us
  transfers between devices with their start and end apart: 4, of which 3 were waited for; matrix products, arithmetic and copies ran while one was open for 1% of the time, Pallas kernels for 0%

commit v1 on v0

--- a/solution.py
+++ b/solution.py
@@ -37,7 +37,9 @@
     norm_diff = outer_norms - inner_norms[0]
     moved = lax.all_to_all(inner_attn[0], "shard", split_axis=1, concat_axis=0, tiled=True)
     attn_term = outer_attn - moved
-    coeff_sum = lax.psum(partial_coeff, ("group", "shard"))
+    coeff_sum = partial_coeff
+    for axis in ("shard", "group"):
+        coeff_sum = lax.psum(coeff_sum, axis)
     attn_sum, norm_sum = lax.psum((attn_term, norm_diff), "group")
     attn_delta = attn_sum / groups
     norm_delta = norm_sum / groups

time: 639 us -> 1220 us (1.91)
  waiting for transfers between devices: 540 us -> 1130 us
    psum x2, waiting for transfers between devices: 523 us -> 1100 us  [on_device(): coeff_sum = lax.psum(coeff_sum, axis)]
    all_to_all x1, waiting for transfers between devices: 0.01 us -> 13.2 us  [on_device(): lax.all_to_all(new_attn.astype(jnp.bfloat16), 'shard', split_axis=0, conc...]
  transfers between devices with their start and end apart: 4 -> 4, of which waited for: 3 -> 4; matrix products, arithmetic and copies ran while one was open for 1% -> 1% of each run, Pallas kernels for 0% -> 0%
where the time goes in v1:
time: 1220 us
  waiting for transfers between devices  1130 us (93%)
  starting transfers between devices  38.2 us (3%)
  blocking collectives  22.7 us (2%)
  between operations  14.2 us (1%)
    psum x2, waiting for transfers between devices, on_device(): coeff_sum = lax.psum(coeff_sum, axis)  1100 us
  transfers between devices with their start and end apart: 4, of which 4 were waited for; matrix products, arithmetic and copies ran while one was open for 1% of the time, Pallas kernels for 0%

profile of v1, /device:TPU:1, one launch (start us, length us, event | category | flops | bytes accessed | tf_op | source)
XLA Modules:
  0.0 1221.4 jit_solution(6836148899837605894)
XLA Ops:
  7.2 0.0 copy-start
  7.2 1.3 reduce
  8.5 0.2 all_to_all.28
  8.7 0.0 copy-start.2
  8.7 0.2 copy.34
  8.9 0.0 copy-start.1
  8.9 1.0 reshape.22
  10.0 22.2 %all-to-all-start = ((f32[64,1,576]{2,1,0:T(1,128)}), f32[64,1,576]{2,1,0:T(1,128)S(1)}, u32[]{:S(2)}, u32[]{:S(2)}) async-start(f32[64,1,576]{2,1,0:T(1,128)} %reshape.22), calls=%async_computation | async-start | bytes 327680 | tf_op jit(solution)/shard_map/all_to_all | solution.py:38
  32.2 0.0 all-reduce.4.cloned.1.call-start
  32.3 0.0 copy-done
  32.3 0.0 copy-done.2
  32.3 0.0 copy-done.1
  32.3 1.3 convolution_bitcast_fusion
  33.6 0.0 copy-start.5
  33.6 0.0 all-reduce.4.cloned.1.call-update
  33.6 0.0 copy-start.6
  33.6 0.0 all-reduce.6.cloned.1.call-start
  33.7 0.8 copy-done.5
  34.5 0.2 copy.29
  34.7 0.0 copy-done.6
  34.7 0.2 copy.28
  34.8 14.9 %all-to-all-done = f32[64,1,576]{2,1,0:T(1,128)S(1)} async-done(((f32[64,1,576]{2,1,0:T(1,128)}), f32[64,1,576]{2,1,0:T(1,128)S(1)}, u32[]{:S(2)}, u32[]{:S(2)}) %all-to-all-start) | async-done | bytes 147488 | tf_op jit(solution)/shard_map/all_to_all | solution.py:38
  49.7 0.5 broadcast.29
  50.3 1.0 reduce.1
  51.3 0.2 reshape.23
  51.6 0.8 sub.20
  52.4 1004.4 %all-reduce.4.cloned.1.call-done = f32[64,768]{1,0:T(8,128)} async-done(((f32[64,768]{1,0:T(8,128)}), f32[64,768]{1,0:T(8,128)}) %all-reduce.4.cloned.1.call-update) | async-done | bytes 196624 | tf_op jit(solution)/shard_map/psum | solution.py:42
  1056.8 0.0 copy-start.7
  1056.8 0.0 copy-start.8
  1056.8 0.0 all-reduce.6.cloned.1.call-update
  1056.8 0.7 copy-done.7
  1057.5 0.0 copy-done.8
  1057.5 0.0 copy-start.9
  1057.5 22.7 %psum.31 = f32[4,12]{1,0:T(4,128)S(1)} all-reduce(f32[4,12]{1,0:T(4,128)S(1)} %bitcast_subtract_fusion.2), channel_id=1, replica_groups=mesh['group'=8,'shard'=64] {'group'}, use_global_device_ids=true, to_apply=%region_3.0 | all-reduce | flops 48 | bytes 384 | tf_op jit(solution)/shard_map/psum | solution.py:43
  1080.2 0.0 copy-done.9
  1080.2 0.6 add_subtract_fusion.2
  1080.8 97.6 %all-reduce.6.cloned.1.call-done = (f32[64,768]{1,0:T(8,128)}, f32[768,48]{1,0:T(8,128)}) async-done(((f32[64,768]{1,0:T(8,128)}, f32[768,48]{1,0:T(8,128)}), (f32[64,768]{1,0:T(8,128)}, f32[768,48]{1,0:T(8,128)})) %all-reduce.6.cloned.1.call-update) | async-done | bytes 344080 | tf_op jit(solution)/shard_map/psum | solution.py:42
  1178.4 1.1 fusion.4
  1179.5 0.1 all_to_all.32
  1179.6 0.0 copy-start.3
  1179.6 0.9 reshape.24
  1180.5 15.8 %all-to-all-start.1 = ((bf16[64,2,288]{2,1,0:T(2,128)(2,1)}), bf16[64,2,288]{2,1,0:T(2,128)(2,1)S(1)}, u32[]{:S(2)}, u32[]{:S(2)}) async-start(bf16[64,2,288]{2,1,0:T(2,128)(2,1)} %reshape.24), calls=%async_computation.1 | async-start | bytes 196608 | tf_op jit(solution)/shard_map/all_to_all | solution.py:53
  1196.4 0.8 copy.31
  1197.2 0.0 copy-start.4
  1197.2 0.8 copy.32
  1198.0 0.0 copy-done.3
  1198.0 0.1 copy-done.4
  1198.1 2.0 add_subtract_fusion
  1200.1 13.2 %all-to-all-done.1 = bf16[64,2,288]{2,1,0:T(2,128)(2,1)S(1)} async-done(((bf16[64,2,288]{2,1,0:T(2,128)(2,1)}), bf16[64,2,288]{2,1,0:T(2,128)(2,1)S(1)}, u32[]{:S(2)}, u32[]{:S(2)}) %all-to-all-start.1) | async-done | bytes 73760 | tf_op jit(solution)/shard_map/all_to_all | solution.py:53
  1213.3 0.2 reshape.25
  1213.6 0.1 copy.30
  1213.6 0.9 all_to_all.35
  (3 shorter events, 0.1 us)
Async XLA Ops:
  7.2 25.1 %copy-start = (f32[240,64]{0,1:T(8,128)S(1)}, f32[240,64]{0,1:T(8,128)}, u32[]{:S(2)}) copy-start(f32[240,64]{0,1:T(8,128)} %param.13) | copy-start | bytes 184324
  8.7 23.6 %copy-start.2 = (f32[1,240,768]{2,1,0:T(8,128)S(1)}, f32[1,240,768]{2,1,0:T(8,128)}, u32[]{:S(2)}) copy-start(f32[1,240,768]{2,1,0:T(8,128)} %param.10) | copy-start | bytes 2211844
  8.9 23.4 %copy-start.1 = (f32[240,768]{1,0:T(8,128)S(1)}, f32[240,768]{1,0:T(8,128)}, u32[]{:S(2)}) copy-start(f32[240,768]{1,0:T(8,128)} %param.11) | copy-start | bytes 2211844
  10.0 39.8 %all-to-all-start = ((f32[64,1,576]{2,1,0:T(1,128)}), f32[64,1,576]{2,1,0:T(1,128)S(1)}, u32[]{:S(2)}, u32[]{:S(2)}) async-start(f32[64,1,576]{2,1,0:T(1,128)} %reshape.22), calls=%async_computation | async-start | bytes 327680 | tf_op jit(solution)/shard_map/all_to_all | solution.py:38
  32.2 1024.6 %all-reduce.4.cloned.1.call-start = ((), (), s32[]{:S(2)}) async-start(), calls=%async_computation.2 | async-start | bytes 393216 | tf_op jit(solution)/shard_map/psum | solution.py:42
  33.6 0.9 copy-start.5
  33.6 1.1 copy-start.6
  33.6 1144.8 %all-reduce.6.cloned.1.call-start = ((), (), s32[]{:S(2)}) async-start(), calls=%async_computation.3 | async-start | bytes 1179648 | tf_op jit(solution)/shard_map/psum | solution.py:42
  1056.8 0.7 copy-start.7
  1056.8 0.7 copy-start.8
  1057.5 22.7 %copy-start.9 = (f32[4,12]{1,0:T(4,128)S(1)}, f32[4,12]{1,0:T(4,128)}, u32[]{:S(2)}) copy-start(f32[4,12]{1,0:T(4,128)} %param.19) | copy-start | bytes 580
  1179.6 18.4 %copy-start.3 = (f32[240,768]{1,0:T(8,128)S(1)}, f32[240,768]{1,0:T(8,128)}, u32[]{:S(2)}) copy-start(f32[240,768]{1,0:T(8,128)} %param.12) | copy-start | bytes 2211844
  1180.5 32.8 %all-to-all-start.1 = ((bf16[64,2,288]{2,1,0:T(2,128)(2,1)}), bf16[64,2,288]{2,1,0:T(2,128)(2,1)S(1)}, u32[]{:S(2)}, u32[]{:S(2)}) async-start(bf16[64,2,288]{2,1,0:T(2,128)(2,1)} %reshape.24), calls=%async_computation.1 | async-start | bytes 196608 | tf_op jit(solution)/shard_map/all_to_all | solution.py:53
  1197.2 0.9 copy-start.4
Sparse Core Ops, SparseCore 0:
  36.5 1020.1 all-reduce.3
  1060.6 117.7 all-reduce.5
